TPU v7x, 256 devices: a whole 4x4x8 slice. The times are simulated.
256 devices in a mesh: row: 8 (over x, core), col: 32 (over y, z).
Axes of the slice: x: 4, y: 4, z: 8, core: 2. Of those that a mesh axis runs over, the one named last changes fastest.
Arguments:
- matrix: float32 [16384, 16384], P('row', 'col'), as said below
- panel: float32 [16384, 256], P(('row', 'col')), may hold values from -0.046875 to 0.046875
- factor: float32 [256, 256], replicated, as said below
Outputs:
- updated: float32 [16384, 16384], P('row', 'col')
- correction: float32 [16384, 256], P(('row', 'col'))
Inputs may be any that keep to these rules, and one draw needn't show every extreme that they name: `matrix`: symmetric. `factor`: upper triangular with a positive diagonal.
All inputs are finite; a program needn't handle non-finite values.
Results may differ from a plain program's by a relative error of at most 0.000071.
Values sent between devices are 32-bit elements; how exact they have to be, the bound alone decides.
No kernel may reach another device: no remote copies, remote signals or barrier semaphores. Data moves between devices by JAX's collectives and lax.ppermute only.
A program may use at most 64 MiB of HBM per device.

v0:
```python
import jax
import jax.numpy as jnp
from jax import lax
from jax.sharding import PartitionSpec as P


def from_root(value, axis, source):
    kept = jnp.where(lax.axis_index(axis) == source, value, 0).astype(value.dtype)
    return lax.psum(kept, axis)


def mult(left, right):
    return jnp.dot(left, right, precision=lax.Precision.HIGHEST, preferred_element_type=jnp.float32)


def per_device(matrix, panel, factor):
    ncols = lax.axis_size("col")
    nrows = lax.axis_size("row")
    blocks = panel.shape[0]
    col_index = lax.axis_index("col")
    col_rows = blocks * nrows
    offset = col_index * nrows % ncols * blocks
    owner = col_index * nrows // ncols
    row_panel = lax.all_gather(panel, "col", axis=0, tiled=True)
    col_panel = from_root(lax.dynamic_slice_in_dim(row_panel, offset, col_rows, 0), "row", owner)
    product = lax.psum_scatter(mult(matrix, col_panel), "col", scatter_dimension=0, tiled=True)
    scaled = mult(product, factor)
    small = lax.psum(mult(panel.T, scaled), ("row", "col"))
    correction = scaled - 0.5 * mult(panel, mult(factor.T, small))
    row_corr = lax.all_gather(correction, "col", axis=0, tiled=True)
    col_corr = from_root(lax.dynamic_slice_in_dim(row_corr, offset, col_rows, 0), "row", owner)
    updated = matrix - mult(row_panel, col_corr.T) - mult(row_corr, col_panel.T)
    return (updated, correction)


def solution(mesh):
    in_specs = (P("row", "col"), P(("row", "col"), None), P())
    out_specs = (P("row", "col"), P(("row", "col"), None))
    return jax.shard_map(
        per_device, mesh=mesh, in_specs=in_specs, out_specs=out_specs, check_vma=False
    )
```

profile of v0, /device:TPU:8, one launch (start us, length us, event | category | flops | bytes accessed | tf_op | source)
XLA Modules:
  0.0 802.7 jit_solution(14840826598810947577)
XLA Ops:
  7.2 0.0 copy-start
  7.2 0.0 all-gather.3.cloned.1.call-start
  7.2 0.7 all-gather.3.cloned.1.call-update
  7.9 0.0 all-reduce.4.cloned.1.call-start
  8.0 82.3 %all-gather.3.cloned.1.call-done = f32[2048,256]{1,0:T(8,128)} async-done(((f32[64,256]{1,0:T(8,128)}), f32[2048,256]{1,0:T(8,128)}) %all-gather.3.cloned.1.call-update) | async-done | bytes 2097168 | tf_op jit(solution)/shard_map/all_gather | solution.py:24
  90.3 1.9 dynamic-slice_select_fusion.1
  92.1 0.0 all-reduce.4.cloned.1.call-update
  92.2 0.0 reduce-scatter.4.cloned.1.call-start
  92.2 65.1 %all-reduce.4.cloned.1.call-done = f32[512,256]{1,0:T(8,128)} async-done(((f32[512,256]{1,0:T(8,128)}), f32[512,256]{1,0:T(8,128)}) %all-reduce.4.cloned.1.call-update) | async-done | bytes 524304 | tf_op jit(solution)/shard_map/psum | solution.py:9
  157.3 8.7 %convolution_bitcast_fusion = f32[2048,256]{0,1:T(8,128)S(1)} fusion(f32[512,256]{1,0:T(8,128)} %all-reduce.4.cloned.1.call-done, f32[2048,512]{1,0:T(8,128)} %param.3), kind=kOutput, calls=%fused_computation.2 | convolution fusion | flops 3221225472 | bytes 6815744 | tf_op jit(solution)/shard_map/dot_general | solution.py:13
  166.0 0.0 copy-start.3
  166.0 1.8 copy.12
  167.8 0.0 reduce-scatter.4.cloned.1.call-update
  167.8 0.0 all-reduce.6.cloned.1.call-start
  167.9 214.8 %reduce-scatter.4.cloned.1.call-done = f32[64,256]{1,0:T(8,128)} async-done(((f32[2048,256]{1,0:T(8,128)}), f32[64,256]{1,0:T(8,128)}) %reduce-scatter.4.cloned.1.call-update) | async-done | bytes 65552
  382.7 1.1 fusion.3
  383.8 1.1 convolution_bitcast_fusion.1
  384.9 0.0 all-reduce.6.cloned.1.call-update
  384.9 0.0 all-gather.5.cloned.1.call-start
  385.0 252.9 %all-reduce.6.cloned.1.call-done = f32[256,256]{0,1:T(8,128)} async-done(((f32[256,256]{0,1:T(8,128)}), f32[256,256]{0,1:T(8,128)}) %all-reduce.6.cloned.1.call-update) | async-done | bytes 262160 | tf_op jit(solution)/shard_map/psum | solution.py:28
  637.9 1.3 fusion.4
  639.2 1.0 fusion.2
  640.3 0.0 all-gather.5.cloned.1.call-update
  640.3 0.0 all-reduce.8.cloned.1.call-start
  640.3 5.4 copy.8
  645.8 70.7 %all-gather.5.cloned.1.call-done = f32[2048,256]{1,0:T(8,128)} async-done(((f32[64,256]{1,0:T(8,128)}), f32[2048,256]{1,0:T(8,128)}) %all-gather.5.cloned.1.call-update) | async-done | bytes 2097168 | tf_op jit(solution)/shard_map/all_gather | solution.py:30
  716.5 1.9 dynamic-slice_select_fusion
  718.4 0.0 all-reduce.8.cloned.1.call-update
  718.4 6.9 fusion.5
  725.3 57.5 %all-reduce.8.cloned.1.call-done = f32[512,256]{1,0:T(8,128)} async-done(((f32[512,256]{1,0:T(8,128)}), f32[512,256]{1,0:T(8,128)}) %all-reduce.8.cloned.1.call-update) | async-done | bytes 524304 | tf_op jit(solution)/shard_map/psum | solution.py:9
  782.8 7.7 fusion
  790.5 5.3 copy.10
  (6 shorter events, 0.0 us)
Async XLA Ops:
  7.2 375.5 %copy-start = (f32[256,256]{1,0:T(8,128)S(1)}, f32[256,256]{1,0:T(8,128)}, u32[]{:S(2)}) copy-start(f32[256,256]{1,0:T(8,128)} %param.5) | copy-start | bytes 786436
  7.2 83.1 %all-gather.3.cloned.1.call-start = ((), (), s32[]{:S(2)}) async-start(), calls=%async_computation.1 | async-start | bytes 2162688 | tf_op jit(solution)/shard_map/all_gather | solution.py:24
  7.9 149.4 %all-reduce.4.cloned.1.call-start = ((), (), s32[]{:S(2)}) async-start(), calls=%async_computation.2 | async-start | bytes 1048576 | tf_op jit(solution)/shard_map/psum | solution.py:9
  92.2 290.5 %reduce-scatter.4.cloned.1.call-start = ((), (), s32[]{:S(2)}) async-start(), calls=%async_computation.6 | async-start | bytes 2162688
  166.0 217.8 %copy-start.3 = (f32[64,256]{1,0:T(8,128)S(1)}, f32[64,256]{1,0:T(8,128)}, u32[]{:S(2)}) copy-start(f32[64,256]{1,0:T(8,128)} %param.4) | copy-start | bytes 196612
  167.8 470.1 %all-reduce.6.cloned.1.call-start = ((), (), s32[]{:S(2)}) async-start(), calls=%async_computation.3 | async-start | bytes 524288 | tf_op jit(solution)/shard_map/psum | solution.py:28
  384.9 331.5 %all-gather.5.cloned.1.call-start = ((), (), s32[]{:S(2)}) async-start(), calls=%async_computation.4 | async-start | bytes 2162688 | tf_op jit(solution)/shard_map/all_gather | solution.py:30
  640.3 78.1 %copy-start.2 = (f32[512,256]{1,0:T(8,128)S(1)}, f32[512,256]{1,0:T(8,128)}, u32[]{:S(2)}) copy-start(f32[512,256]{1,0:T(8,128)} %all-reduce.4.cloned.1.call-done) | copy-start | bytes 1572868
  640.3 142.5 %all-reduce.8.cloned.1.call-start = ((), (), s32[]{:S(2)}) async-start(), calls=%async_computation.5 | async-start | bytes 1048576 | tf_op jit(solution)/shard_map/psum | solution.py:9
  645.8 137.0 %copy-start.1 = (f32[2048,256]{1,0:T(8,128)S(1)}, f32[2048,256]{1,0:T(8,128)}, u32[]{:S(2)}) copy-start(f32[2048,256]{1,0:T(8,128)} %all-gather.3.cloned.1.call-done) | copy-start | bytes 6291460
Sparse Core Ops, SparseCore 0:
  10.6 79.6 all-gather.2
  93.2 64.0 all-reduce.3
  168.0 214.6 reduce-scatter.3
  388.6 249.2 all-reduce.5
  640.9 75.5 all-gather.4
  718.7 64.0 all-reduce.7
where the time goes:
time: 803 us
  waiting for transfers between devices  744 us (93%)
  matrix products  27.9 us (3%)
  between operations  14.2 us (2%)
  local copies, waits for them, and re-layouts  12.6 us (2%)
    psum x1, waiting for transfers between devices, per_device(): small = lax.psum(mult(panel.T, scaled), ('row', 'col'))  253 us
    unnamed x7, waiting for transfers between devices  216 us
    psum x2, waiting for transfers between devices, from_root(): return lax.psum(kept, axis)  123 us
    all_gather x1, waiting for transfers between devices, per_device(): row_panel = lax.all_gather(panel, 'col', axis=0, tiled=True)  82.3 us
    all_gather x1, waiting for transfers between devices, per_device(): row_corr = lax.all_gather(correction, 'col', axis=0, tiled=True)  70.7 us
    dot_general x7, matrix products, mult(): jnp.dot(left, right, precision=lax.Precision.HIGHEST, preferred_element_t...  27.9 us
  transfers between devices with their start and end apart: 6, of which 6 were waited for; matrix products, arithmetic and copies ran while one was open for 2% of the time, Pallas kernels for 0%

commit v1 on v0

--- a/solution.py
+++ b/solution.py
@@ -25,7 +25,7 @@
     col_panel = from_root(lax.dynamic_slice_in_dim(row_panel, offset, col_rows, 0), "row", owner)
     product = lax.psum_scatter(mult(matrix, col_panel), "col", scatter_dimension=0, tiled=True)
     scaled = mult(product, factor)
-    small = lax.psum(mult(panel.T, scaled), ("row", "col"))
+    small = lax.psum(lax.psum(mult(panel.T, scaled), "row"), "col")
     correction = scaled - 0.5 * mult(panel, mult(factor.T, small))
     row_corr = lax.all_gather(correction, "col", axis=0, tiled=True)
     col_corr = from_root(lax.dynamic_slice_in_dim(row_corr, offset, col_rows, 0), "row", owner)

time: 803 us -> 761 us (0.948)
  waiting for transfers between devices: 744 us -> 701 us
    psum x1 -> x2, waiting for transfers between devices: 253 us -> 210 us  [per_device(): small = lax.psum(lax.psum(mult(panel.T, scaled), 'row'), 'col')]
    unnamed x7 -> x8, waiting for transfers between devices: 216 us -> 216 us
  transfers between devices with their start and end apart: 6 -> 7, of which waited for: 6 -> 7; matrix products, arithmetic and copies ran while one was open for 2% -> 2% of each run, Pallas kernels for 0% -> 0%
where the time goes in v1:
time: 761 us; the launch traced here: 760 us
  waiting for transfers between devices  701 us (92%)
  matrix products  27.9 us (4%)
  between operations  14.2 us (2%)
  local copies, waits for them, and re-layouts  12.6 us (2%)
    unnamed x8, waiting for transfers between devices  216 us
    psum x2, waiting for transfers between devices, per_device(): small = lax.psum(lax.psum(mult(panel.T, scaled), 'row'), 'col')  210 us
    psum x2, waiting for transfers between devices, from_root(): return lax.psum(kept, axis)  123 us
    all_gather x1, waiting for transfers between devices, per_device(): row_panel = lax.all_gather(panel, 'col', axis=0, tiled=True)  82.3 us
    all_gather x1, waiting for transfers between devices, per_device(): row_corr = lax.all_gather(correction, 'col', axis=0, tiled=True)  70.4 us
    dot_general x7, matrix products, mult(): jnp.dot(left, right, precision=lax.Precision.HIGHEST, preferred_element_t...  27.9 us
  transfers between devices with their start and end apart: 7, of which 7 were waited for; matrix products, arithmetic and copies ran while one was open for 2% of the time, Pallas kernels for 0%

profile of v1, /device:TPU:8, one launch (start us, length us, event | category | flops | bytes accessed | tf_op | source)
XLA Modules:
  0.0 760.2 jit_solution(13323789430808149989)
XLA Ops:
  7.2 0.0 all-gather.3.cloned.1.call-start
  7.2 0.7 all-gather.3.cloned.1.call-update
  7.9 0.0 all-reduce.5.cloned.1.call-start
  8.0 82.3 %all-gather.3.cloned.1.call-done = f32[2048,256]{1,0:T(8,128)} async-done(((f32[64,256]{1,0:T(8,128)}), f32[2048,256]{1,0:T(8,128)}) %all-gather.3.cloned.1.call-update) | async-done | bytes 2097168 | tf_op jit(solution)/shard_map/all_gather | solution.py:24
  90.3 1.9 dynamic-slice_select_fusion.1
  92.1 0.0 all-reduce.5.cloned.1.call-update
  92.2 0.0 reduce-scatter.4.cloned.1.call-start
  92.2 65.1 %all-reduce.5.cloned.1.call-done = f32[512,256]{1,0:T(8,128)} async-done(((f32[512,256]{1,0:T(8,128)}), f32[512,256]{1,0:T(8,128)}) %all-reduce.5.cloned.1.call-update) | async-done | bytes 524304 | tf_op jit(solution)/shard_map/psum | solution.py:9
  157.3 8.7 %convolution_bitcast_fusion = f32[2048,256]{0,1:T(8,128)S(1)} fusion(f32[512,256]{1,0:T(8,128)} %all-reduce.5.cloned.1.call-done, f32[2048,512]{1,0:T(8,128)} %param.3), kind=kOutput, calls=%fused_computation.2 | convolution fusion | flops 3221225472 | bytes 6815744 | tf_op jit(solution)/shard_map/dot_general | solution.py:13
  166.0 1.8 copy.12
  167.8 0.0 reduce-scatter.4.cloned.1.call-update
  167.8 0.0 all-reduce.7.cloned.1.call-start
  167.9 214.8 %reduce-scatter.4.cloned.1.call-done = f32[64,256]{1,0:T(8,128)} async-done(((f32[2048,256]{1,0:T(8,128)}), f32[64,256]{1,0:T(8,128)}) %reduce-scatter.4.cloned.1.call-update) | async-done | bytes 65552
  382.7 1.1 fusion.3
  383.8 1.1 convolution_bitcast_fusion.1
  384.9 0.0 all-reduce.7.cloned.1.call-update
  384.9 0.0 all-reduce.9.cloned.1.call-start
  385.0 64.5 %all-reduce.7.cloned.1.call-done = f32[256,256]{0,1:T(8,128)} async-done(((f32[256,256]{0,1:T(8,128)}), f32[256,256]{0,1:T(8,128)}) %all-reduce.7.cloned.1.call-update) | async-done | bytes 262160 | tf_op jit(solution)/shard_map/psum | solution.py:28
  449.5 0.0 all-gather.5.cloned.1.call-start
  449.6 145.9 %all-reduce.9.cloned.1.call-done = f32[256,256]{0,1:T(8,128)} async-done(((f32[256,256]{0,1:T(8,128)}), f32[256,256]{0,1:T(8,128)}) %all-reduce.9.cloned.1.call-update) | async-done | bytes 262160 | tf_op jit(solution)/shard_map/psum | solution.py:28
  595.5 1.3 fusion.4
  596.8 1.0 fusion.2
  597.8 0.0 all-gather.5.cloned.1.call-update
  597.8 0.0 all-reduce.11.cloned.1.call-start
  597.9 5.4 copy.8
  603.3 70.4 %all-gather.5.cloned.1.call-done = f32[2048,256]{1,0:T(8,128)} async-done(((f32[64,256]{1,0:T(8,128)}), f32[2048,256]{1,0:T(8,128)}) %all-gather.5.cloned.1.call-update) | async-done | bytes 2097168 | tf_op jit(solution)/shard_map/all_gather | solution.py:30
  673.7 1.9 dynamic-slice_select_fusion
  675.6 0.0 all-reduce.11.cloned.1.call-update
  675.6 6.9 fusion.5
  682.6 57.7 %all-reduce.11.cloned.1.call-done = f32[512,256]{1,0:T(8,128)} async-done(((f32[512,256]{1,0:T(8,128)}), f32[512,256]{1,0:T(8,128)}) %all-reduce.11.cloned.1.call-update) | async-done | bytes 524304 | tf_op jit(solution)/shard_map/psum | solution.py:9
  740.3 7.7 %fusion = f32[2048,512]{0,1:T(8,128)} fusion(f32[2048,512]{0,1:T(8,128)} %fusion.5, f32[2048,512]{0,1:T(8,128)} %copy.8, f32[512,256]{1,0:T(8,128)} %all-reduce.11.cloned.1.call-done, f32[2048,256]{1,0:T(8,128)S(1)} %copy-done.1), kind=kOutput, calls=%fused_computation.1 | convolution fusion | flops 3223322624 | bytes 15204352 | tf_op jit(solution)/shard_map/dot_general | solution.py:13
  748.0 5.3 copy.10
  (9 shorter events, 0.0 us)
Async XLA Ops:
  7.2 375.5 %copy-start = (f32[256,256]{1,0:T(8,128)S(1)}, f32[256,256]{1,0:T(8,128)}, u32[]{:S(2)}) copy-start(f32[256,256]{1,0:T(8,128)} %param.5) | copy-start | bytes 786436
  7.2 83.1 %all-gather.3.cloned.1.call-start = ((), (), s32[]{:S(2)}) async-start(), calls=%async_computation.1 | async-start | bytes 2162688 | tf_op jit(solution)/shard_map/all_gather | solution.py:24
  7.9 149.4 %all-reduce.5.cloned.1.call-start = ((), (), s32[]{:S(2)}) async-start(), calls=%async_computation.2 | async-start | bytes 1048576 | tf_op jit(solution)/shard_map/psum | solution.py:9
  92.2 290.5 %reduce-scatter.4.cloned.1.call-start = ((), (), s32[]{:S(2)}) async-start(), calls=%async_computation.7 | async-start | bytes 2162688
  166.0 217.8 %copy-start.3 = (f32[64,256]{1,0:T(8,128)S(1)}, f32[64,256]{1,0:T(8,128)}, u32[]{:S(2)}) copy-start(f32[64,256]{1,0:T(8,128)} %param.4) | copy-start | bytes 196612
  167.8 281.7 %all-reduce.7.cloned.1.call-start = ((), (), s32[]{:S(2)}) async-start(), calls=%async_computation.3 | async-start | bytes 524288 | tf_op jit(solution)/shard_map/psum | solution.py:28
  384.9 210.5 %all-reduce.9.cloned.1.call-start = ((), (), s32[]{:S(2)}) async-start(), calls=%async_computation.4 | async-start | bytes 524288 | tf_op jit(solution)/shard_map/psum | solution.py:28
  449.5 224.2 %all-gather.5.cloned.1.call-start = ((), (), s32[]{:S(2)}) async-start(), calls=%async_computation.5 | async-start | bytes 2162688 | tf_op jit(solution)/shard_map/all_gather | solution.py:30
  597.8 77.8 %copy-start.2 = (f32[512,256]{1,0:T(8,128)S(1)}, f32[512,256]{1,0:T(8,128)}, u32[]{:S(2)}) copy-start(f32[512,256]{1,0:T(8,128)} %all-reduce.5.cloned.1.call-done) | copy-start | bytes 1572868
  597.8 142.5 %all-reduce.11.cloned.1.call-start = ((), (), s32[]{:S(2)}) async-start(), calls=%async_computation.6 | async-start | bytes 1048576 | tf_op jit(solution)/shard_map/psum | solution.py:9
  603.3 137.0 %copy-start.1 = (f32[2048,256]{1,0:T(8,128)S(1)}, f32[2048,256]{1,0:T(8,128)}, u32[]{:S(2)}) copy-start(f32[2048,256]{1,0:T(8,128)} %all-gather.3.cloned.1.call-done) | copy-start | bytes 6291460
Sparse Core Ops, SparseCore 0:
  10.6 79.6 all-gather.2
  93.2 64.0 all-reduce.4
  168.0 214.6 reduce-scatter.3
  385.4 64.0 all-reduce.6
  453.2 142.2 all-reduce.8
  598.8 74.8 all-gather.4
  676.2 64.0 all-reduce.10
